TPU v7x, 32 devices: a whole 2x2x4 slice. The times are simulated.
32 devices in a mesh: dp: 8 (over y, x, core), vocab: 4 (over z).
Axes of the slice: x: 2, y: 2, z: 4, core: 2. Of those that a mesh axis runs over, the one named last changes fastest.
Arguments:
- hidden: bfloat16 [128, 5120], P('dp', 'vocab')
- inputs: bfloat16 [128, 3072], P('dp', 'vocab'), may hold values from -6 to 6
- gain: float32 [5120], replicated, may hold values from 0.5 to 1.5
- unembed: bfloat16 [6400, 5120], P(('dp', 'vocab'))
- proj_out: bfloat16 [5120, 128], replicated, may hold values from -6 to 6
- proj_in: bfloat16 [3072, 128], replicated, may hold values from -0.109375 to 0.109375
- targets: int32 [128], replicated, may hold values from 0 to 6399
- segment_ids: int32 [128], replicated, may hold values from 0 to 3, never falling along the last dimension, each value on 1 to 96 neighbouring positions
- store: bfloat16 [2048, 16384], P(('dp', 'vocab')), may hold values from -0.005859375 to 0.005859375
Outputs:
- scores: float32 [4, 2048], P(None, ('dp', 'vocab'))
- logprob: float32 [128], P('dp')
Inputs may be any that keep to these rules, and one draw needn't show every extreme that they name: `segment_ids`: each sequence is a run of consecutive tokens; ids never fall; each sequence has 1 to 96 tokens and one has exactly 96.
All inputs are finite; a program needn't handle non-finite values.
Results may differ from a plain program's by a relative error of at most 0.0074.
Values may be sent and summed in bfloat16 or wider, within the bound.
No kernel may reach another device: no remote copies, remote signals or barrier semaphores. Data moves between devices by JAX's collectives and lax.ppermute only.
A program may use at most 64 MiB of HBM per device.

v0:
```python
import jax
import jax.numpy as jnp
from jax import lax
from jax.sharding import PartitionSpec as P

D = 5120
V_DEV = 200
PROJ = 128
EPSILON = 1e-06


def body(hidden, inputs, gain, unembed, proj_out, proj_in, targets, segment_ids, store):
    token_count = targets.shape[0]
    seq_count = token_count // 32
    local_rows = hidden.shape[0]
    token_part = lax.all_gather(hidden, "vocab", axis=1, tiled=True)
    gathered = lax.all_gather(token_part, "dp", axis=0, tiled=True)
    hidden_f32 = gathered.astype(jnp.float32)
    root_mean = jnp.sqrt(jnp.mean(hidden_f32 * hidden_f32, axis=1) + EPSILON)
    normed = (hidden_f32 * gain[None, :] / root_mean[:, None]).astype(jnp.bfloat16)
    logits = lax.dot_general(
        normed, unembed, (((1,), (1,)), ((), ())), preferred_element_type=jnp.float32
    )
    device_pos = lax.axis_index("dp") * lax.axis_size("vocab") + lax.axis_index("vocab")
    column_ids = device_pos * V_DEV + jnp.arange(V_DEV, dtype=jnp.int32)
    onehot = targets[:, None] == column_ids[None, :]
    local_peak = jnp.max(logits, axis=1)
    local_target = jnp.sum(jnp.where(onehot, logits, jnp.zeros_like(logits)), axis=1)
    row_peak = lax.pmax(local_peak, ("dp", "vocab"))
    shifted = jnp.exp(logits - row_peak[:, None])
    row_total, target_logit = lax.psum((jnp.sum(shifted, axis=1), local_target), ("dp", "vocab"))
    logprob = target_logit - row_peak - jnp.log(row_total)
    logprob_rows = lax.dynamic_slice_in_dim(logprob, lax.axis_index("dp") * local_rows, local_rows)
    dlogits = (onehot.astype(jnp.float32) - shifted / row_total[:, None]).astype(jnp.bfloat16)
    dnormed = jnp.dot(dlogits, unembed, preferred_element_type=jnp.float32)
    weighted = dnormed * gain[None, :]
    part_proj = jnp.dot(weighted, proj_out.astype(jnp.float32), precision=lax.Precision.HIGHEST)
    part_dot = jnp.sum(weighted * hidden_f32, axis=1)
    grad_proj, grad_dot = lax.psum((part_proj, part_dot), ("dp", "vocab"))
    hidden_proj = jnp.dot(gathered, proj_out, preferred_element_type=jnp.float32)
    out_grad = (
        grad_proj / root_mean[:, None] - hidden_proj * (grad_dot / (D * root_mean**3))[:, None]
    )
    slice_width = inputs.shape[1]
    proj_slice = lax.dynamic_slice_in_dim(
        proj_in, lax.axis_index("vocab") * slice_width, slice_width, 0
    )
    local_proj = jnp.dot(inputs, proj_slice, preferred_element_type=jnp.float32)
    summed_proj = lax.psum(local_proj, "vocab")
    in_proj = lax.all_gather(summed_proj, "dp", axis=0, tiled=True)
    member = (segment_ids[:, None] == jnp.arange(seq_count, dtype=jnp.int32)[None, :]).astype(
        jnp.float32
    )
    spread = (member[:, :, None] * out_grad[:, None, :]).reshape(token_count, seq_count * PROJ)
    seq_grads = lax.dot_general(
        spread, in_proj, (((0,), (0,)), ((), ())), precision=lax.Precision.HIGHEST
    )
    seq_grads = seq_grads.reshape(seq_count, PROJ * PROJ).astype(jnp.bfloat16)
    scores = lax.dot_general(
        seq_grads, store, (((1,), (1,)), ((), ())), preferred_element_type=jnp.float32
    )
    return (scores, logprob_rows)


def solution(mesh):
    in_specs = (
        P("dp", "vocab"),
        P("dp", "vocab"),
        P(),
        P(("dp", "vocab"), None),
        P(),
        P(),
        P(),
        P(),
        P(("dp", "vocab"), None),
    )
    out_specs = (P(None, ("dp", "vocab")), P("dp"))
    return jax.shard_map(body, mesh=mesh, in_specs=in_specs, out_specs=out_specs, check_vma=False)
```

profile of v0, /device:TPU:1, one launch (start us, length us, event | category | flops | bytes accessed | tf_op | source)
XLA Modules:
  0.0 315.6 jit_solution(14063403829248417648)
XLA Ops:
  7.2 0.0 copy-start
  7.2 0.0 copy-start.4
  7.2 0.0 all-gather.2.cloned.1.call-start
  7.2 13.9 %all_gather.9 = bf16[16,5120]{1,0:T(8,128)(2,1)} all-gather(bf16[16,1280]{1,0:T(8,128)(2,1)} %param.9), channel_id=1, replica_groups=mesh['dp'=8,'vocab'=4] {'vocab'}, dimensions={1}, use_global_device_ids=true | all-gather | bytes 204800 | tf_op jit(solution)/shard_map/all_gather | solution.py:16
  21.2 0.0 all-gather.2.cloned.1.call-update
  21.2 0.0 all-reduce.3.cloned.1.call-start
  21.3 1.1 convolution_bitcast_fusion
  22.3 8.7 %psum.38 = f32[16,128]{1,0:T(8,128)S(1)} all-reduce(f32[16,128]{1,0:T(8,128)S(1)} %convolution_bitcast_fusion), channel_id=1, replica_groups=mesh['dp'=8,'vocab'=4] {'vocab'}, use_global_device_ids=true, to_apply=%region_8.9 | all-reduce | flops 2048 | bytes 16384 | tf_op jit(solution)/shard_map/psum | solution.py:49
  31.0 15.7 %all_gather.11 = f32[128,128]{1,0:T(8,128)} all-gather(f32[16,128]{1,0:T(8,128)S(1)} %psum.38), channel_id=1, replica_groups=mesh['dp'=8,'vocab'=4] {'dp'}, dimensions={0}, use_global_device_ids=true | all-gather | bytes 73728 | tf_op jit(solution)/shard_map/all_gather | solution.py:50
  46.8 1.4 fusion.14
  48.1 1.0 all-gather.2.cloned.1.call-done
  49.1 1.6 fusion.2
  50.8 0.0 copy-done.4
  50.8 0.0 copy-start.5
  50.8 0.0 copy-start.1
  50.8 2.9 fusion.23
  53.7 38.0 %pmax.7 = f32[128]{0:T(128)S(1)} all-reduce(f32[128]{0:T(128)S(1)} %get-tuple-element.6), channel_id=1, replica_groups=mesh['dp'=8,'vocab'=4] {'dp','vocab'}, use_global_device_ids=true, to_apply=%region_2.3 | all-reduce | flops 128 | bytes 1024 | tf_op jit(solution)/shard_map/pmax | solution.py:29
  91.7 0.0 copy-done.5
  91.7 0.6 fusion.12
  92.3 41.1 %psum.35 = f32[128]{0:T(128)S(1)} all-reduce(f32[128]{0:T(128)} %get-tuple-element.3), channel_id=1, replica_groups=mesh['dp'=8,'vocab'=4] {'dp','vocab'}, use_global_device_ids=true, to_apply=%region_4.5 | all-reduce | flops 128 | bytes 1024 | tf_op jit(solution)/shard_map/psum | solution.py:31
  133.5 4.3 %fusion.3 = (f32[128]{0:T(128)}, f32[128,5120]{1,0:T(8,128)}) fusion(bf16[128,5120]{1,0:T(8,128)(2,1)S(1)} %copy-done.1, f32[5120]{0:T(1024)S(1)} %copy-done.4, bf16[200,5120]{1,0:T(8,128)(2,1)} %param.12, f32[128,200]{0,1:T(8,128)S(1)} %get-tuple-element.7, f32[128]{0:T(128)S(1)} %psum.35, f32[128]{0:T(128)S(1)} %pmax.7, s32[128]{0:T(128)S(1)} %copy-done.5, ...), kind=kOutput, calls=%fused_computation.7 | convolution fusion | flops 264918912 | bytes 6105888 | tf_op jit(solution)/shard_map/dot_general | solution.py:35
  137.8 39.5 %all-reduce = (f32[128]{0:T(128)}, f32[128]{0:T(128)S(1)}) all-reduce(f32[128]{0:T(128)} %get-tuple-element.8, f32[128]{0:T(128)} %get-tuple-element.2), channel_id=1, replica_groups=mesh['dp'=8,'vocab'=4] {'dp','vocab'}, use_global_device_ids=true, to_apply=%region_7.8 | all-reduce | flops 256 | bytes 2048 | tf_op jit(solution)/shard_map/psum | solution.py:39
  177.2 0.5 log_subtract_fusion
  177.7 4.1 %fusion.24 = f32[128,128]{1,0:T(8,128)} fusion(f32[128,5120]{1,0:T(8,128)} %get-tuple-element.9, bf16[5120,128]{1,0:T(8,128)(2,1)} %param.13), kind=kOutput, calls=%fused_computation.38 | convolution fusion | flops 1006632960 | bytes 3997696 | tf_op jit(solution)/shard_map/dot_general | solution.py:37
  181.9 0.0 all-reduce.3.cloned.1.call-update
  181.9 0.7 fusion.21
  182.6 0.6 dynamic_slice.7
  183.2 121.7 %all-reduce.3.cloned.1.call-done = f32[128,128]{1,0:T(8,128)} async-done(((f32[128,128]{1,0:T(8,128)}), f32[128,128]{1,0:T(8,128)}) %all-reduce.3.cloned.1.call-update) | async-done | bytes 65552 | tf_op jit(solution)/shard_map/psum | solution.py:39
  304.9 1.8 fusion.6
  306.7 0.2 broadcast_multiply_fusion
  306.9 0.6 convolution_convert_fusion
  307.6 1.2 fusion.25
  (11 shorter events, 0.1 us)
Async XLA Ops:
  7.2 300.4 %copy-start = (bf16[64,16384]{1,0:T(8,128)(2,1)S(1)}, bf16[64,16384]{1,0:T(8,128)(2,1)}, u32[]{:S(2)}) copy-start(bf16[64,16384]{1,0:T(8,128)(2,1)} %param.17) | copy-start | bytes 6291460
  7.2 43.6 %copy-start.4 = (f32[5120]{0:T(1024)S(1)}, f32[5120]{0:T(1024)}, u32[]{:S(2)}) copy-start(f32[5120]{0:T(1024)} %param.11) | copy-start | bytes 61444
  7.2 41.9 %all-gather.2.cloned.1.call-start = ((), (), s32[]{:S(2)}) async-start(), calls=%async_computation | async-start | bytes 1474560 | tf_op jit(solution)/shard_map/all_gather | solution.py:17
  21.2 283.7 %all-reduce.3.cloned.1.call-start = ((), (), s32[]{:S(2)}) async-start(), calls=%async_computation.1 | async-start | bytes 131072 | tf_op jit(solution)/shard_map/psum | solution.py:39
  50.8 40.9 %copy-start.5 = (s32[128]{0:T(128)S(1)}, s32[128]{0:T(128)}, u32[]{:S(2)}) copy-start(s32[128]{0:T(128)} %param.15) | copy-start | bytes 1540
  50.8 82.7 %copy-start.1 = (bf16[128,5120]{1,0:T(8,128)(2,1)S(1)}, bf16[128,5120]{1,0:T(8,128)(2,1)}, u32[]{:S(2)}) copy-start(bf16[128,5120]{1,0:T(8,128)(2,1)} %all-gather.2.cloned.1.call-done) | copy-start | bytes 3932164
  177.7 4.8 %copy-start.6 = (f32[128]{0:T(128)S(1)}, f32[128]{0:T(128)}, u32[]{:S(2)}) copy-start(f32[128]{0:T(128)} %log_subtract_fusion) | copy-start | bytes 1540
  181.8 124.8 %copy-start.3 = (f32[128,4]{1,0:T(8,128)S(1)}, f32[128,4]{1,0:T(8,128)}, u32[]{:S(2)}) copy-start(f32[128,4]{1,0:T(8,128)} %fusion.14) | copy-start | bytes 6148
  181.8 125.0 %copy-start.2 = (f32[128,128]{1,0:T(8,128)S(1)}, f32[128,128]{1,0:T(8,128)}, u32[]{:S(2)}) copy-start(f32[128,128]{1,0:T(8,128)} %all_gather.11) | copy-start | bytes 196612
Sparse Core Ops, SparseCore 0:
  21.3 27.7 all-gather.1
  182.0 122.8 all-reduce.2
where the time goes:
time: 316 us
  blocking collectives  157 us (50%)
  waiting for transfers between devices  123 us (39%)
  matrix products  16 us (5%)
  between operations  14.2 us (4%)
  other arithmetic  5.06 us (2%)
    psum x1, waiting for transfers between devices, body(): grad_proj, grad_dot = lax.psum((part_proj, part_dot), ('dp', 'vocab'))  122 us
    psum x1, blocking collectives, body(): lax.psum((jnp.sum(shifted, axis=1), local_target), ('dp', 'vocab'))  41.1 us
    psum x1, blocking collectives, body(): grad_proj, grad_dot = lax.psum((part_proj, part_dot), ('dp', 'vocab'))  39.5 us
    pmax x1, blocking collectives, body(): row_peak = lax.pmax(local_peak, ('dp', 'vocab'))  38 us
    all_gather x1, blocking collectives, body(): in_proj = lax.all_gather(summed_proj, 'dp', axis=0, tiled=True)  15.7 us
    all_gather x1, blocking collectives, body(): token_part = lax.all_gather(hidden, 'vocab', axis=1, tiled=True)  13.9 us
    psum x1, blocking collectives, body(): summed_proj = lax.psum(local_proj, 'vocab')  8.68 us
  transfers between devices with their start and end apart: 2, of which 2 were waited for; matrix products, arithmetic and copies ran while one was open for 1% of the time, Pallas kernels for 0%

commit v1 on v0

--- a/solution.py
+++ b/solution.py
@@ -28,7 +28,9 @@
     local_target = jnp.sum(jnp.where(onehot, logits, jnp.zeros_like(logits)), axis=1)
     row_peak = lax.pmax(local_peak, ("dp", "vocab"))
     shifted = jnp.exp(logits - row_peak[:, None])
-    row_total, target_logit = lax.psum((jnp.sum(shifted, axis=1), local_target), ("dp", "vocab"))
+    row_total, target_logit = lax.psum(
+        lax.psum((jnp.sum(shifted, axis=1), local_target), "vocab"), axis_name="dp"
+    )
     logprob = target_logit - row_peak - jnp.log(row_total)
     logprob_rows = lax.dynamic_slice_in_dim(logprob, lax.axis_index("dp") * local_rows, local_rows)
     dlogits = (onehot.astype(jnp.float32) - shifted / row_total[:, None]).astype(jnp.bfloat16)

time: 316 us -> 297 us (0.940)
  blocking collectives: 157 us -> 125 us
  waiting for transfers between devices: 123 us -> 137 us
    psum x1, blocking collectives: 41.1 us -> 15.9 us  [body(): lax.psum(lax.psum((jnp.sum(shifted, axis=1), local_target), 'vocab'), axi...]
    all_gather x1, waiting for transfers between devices: 0.98 us -> 25.3 us  [body(): gathered = lax.all_gather(token_part, 'dp', axis=0, tiled=True)]
    psum x1, waiting for transfers between devices: 122 us -> 112 us  [body(): grad_proj, grad_dot = lax.psum((part_proj, part_dot), ('dp', 'vocab'))]
    all_gather x1, blocking collectives: 15.7 us -> 11.3 us  [body(): in_proj = lax.all_gather(summed_proj, 'dp', axis=0, tiled=True)]
    psum x1, blocking collectives: 39.5 us -> 36.2 us  [body(): grad_proj, grad_dot = lax.psum((part_proj, part_dot), ('dp', 'vocab'))]
where the time goes in v1:
time: 297 us
  waiting for transfers between devices  137 us (46%)
  blocking collectives  125 us (42%)
  matrix products  16 us (5%)
  between operations  14.2 us (5%)
  other arithmetic  3.87 us (1%)
    psum x1, waiting for transfers between devices, body(): grad_proj, grad_dot = lax.psum((part_proj, part_dot), ('dp', 'vocab'))  112 us
    pmax x1, blocking collectives, body(): row_peak = lax.pmax(local_peak, ('dp', 'vocab'))  38.3 us
    psum x1, blocking collectives, body(): grad_proj, grad_dot = lax.psum((part_proj, part_dot), ('dp', 'vocab'))  36.2 us
    all_gather x1, waiting for transfers between devices, body(): gathered = lax.all_gather(token_part, 'dp', axis=0, tiled=True)  25.3 us
    psum x1, blocking collectives, body(): lax.psum(lax.psum((jnp.sum(shifted, axis=1), local_target), 'vocab'), axi...  15.9 us
    all_gather x1, blocking collectives, body(): token_part = lax.all_gather(hidden, 'vocab', axis=1, tiled=True)  13.9 us
    all_gather x1, blocking collectives, body(): in_proj = lax.all_gather(summed_proj, 'dp', axis=0, tiled=True)  11.3 us
    psum x1, blocking collectives, body(): summed_proj = lax.psum(local_proj, 'vocab')  9.52 us
  transfers between devices with their start and end apart: 2, of which 2 were waited for; matrix products, arithmetic and copies ran while one was open for 1% of the time, Pallas kernels for 0%

profile of v1, /device:TPU:1, one launch (start us, length us, event | category | flops | bytes accessed | tf_op | source)
XLA Modules:
  0.0 297.0 jit_solution(1838450184745530539)
XLA Ops:
  7.2 0.0 copy-start
  7.2 0.0 all-gather.2.cloned.1.call-start
  7.2 13.9 %all_gather.9 = bf16[16,5120]{1,0:T(8,128)(2,1)} all-gather(bf16[16,1280]{1,0:T(8,128)(2,1)} %param.9), channel_id=1, replica_groups=mesh['dp'=8,'vocab'=4] {'vocab'}, dimensions={1}, use_global_device_ids=true | all-gather | bytes 204800 | tf_op jit(solution)/shard_map/all_gather | solution.py:16
  21.2 0.0 all-gather.2.cloned.1.call-update
  21.2 0.0 all-reduce.4.cloned.1.call-start
  21.2 1.1 convolution_bitcast_fusion
  22.3 1.4 fusion.14
  23.7 25.3 %all-gather.2.cloned.1.call-done = bf16[128,5120]{1,0:T(8,128)(2,1)} async-done(((bf16[16,5120]{1,0:T(8,128)(2,1)}), bf16[128,5120]{1,0:T(8,128)(2,1)}) %all-gather.2.cloned.1.call-update) | async-done | bytes 1310736 | tf_op jit(solution)/shard_map/all_gather | solution.py:17
  49.0 1.6 fusion.2
  50.7 0.0 copy-start.4
  50.7 0.0 copy-start.3
  50.7 3.4 %fusion.23 = (f32[128]{0:T(128)}, f32[128,200]{0,1:T(8,128)S(1)}) fusion(bf16[200,5120]{1,0:T(8,128)(2,1)} %param.12, bf16[128,5120]{1,0:T(8,128)(2,1)} %all-gather.2.cloned.1.call-done, f32[128]{0:T(128)S(1)} %add_sqrt_fusion, f32[5120]{0:T(1024)} %param.11), kind=kOutput, calls=%fused_computation.37 | convolution fusion | flops 264790912 | bytes 3482624 | tf_op jit(solution)/shard_map/dot_general | solution.py:21
  54.1 38.3 %pmax.7 = f32[128]{0:T(128)S(1)} all-reduce(f32[128]{0:T(128)} %get-tuple-element.9), channel_id=1, replica_groups=mesh['dp'=8,'vocab'=4] {'dp','vocab'}, use_global_device_ids=true, to_apply=%region_2.3 | all-reduce | flops 128 | bytes 1024 | tf_op jit(solution)/shard_map/pmax | solution.py:29
  92.4 0.0 copy-done.4
  92.4 0.6 fusion.12
  93.0 9.5 %all-reduce.1 = (f32[16,128]{1,0:T(8,128)S(1)}, f32[128]{0:T(128)}, f32[128]{0:T(128)}) all-reduce(f32[16,128]{1,0:T(8,128)S(1)} %convolution_bitcast_fusion, f32[128]{0:T(128)} %get-tuple-element.3, f32[128]{0:T(128)} %get-tuple-element.2), channel_id=1, replica_groups=mesh['dp'=8,'vocab'=4] {'vocab'}, use_global_device_ids=true, to_apply=%region_9.10 | all-reduce | flops 2304 | bytes 18432 | tf_op jit(solution)/shard_map/psum | solution.py:51
  102.6 15.9 %all-reduce = (f32[128]{0:T(128)S(1)}, f32[128]{0:T(128)}) all-reduce(f32[128]{0:T(128)} %get-tuple-element.7, f32[128]{0:T(128)} %get-tuple-element.8), channel_id=1, replica_groups=mesh['dp'=8,'vocab'=4] {'dp'}, use_global_device_ids=true, to_apply=%region_5.6 | all-reduce | flops 256 | bytes 2048 | tf_op jit(solution)/shard_map/psum | solution.py:31
  118.5 0.0 copy-done.1
  118.5 3.8 %fusion.3 = (f32[128]{0:T(128)S(1)}, f32[128,5120]{1,0:T(8,128)}) fusion(bf16[128,5120]{1,0:T(8,128)(2,1)S(1)} %copy-done.1, f32[5120]{0:T(1024)S(1)} %copy-done.3, bf16[200,5120]{1,0:T(8,128)(2,1)} %param.12, f32[128,200]{0,1:T(8,128)S(1)} %get-tuple-element.10, f32[128]{0:T(128)S(1)} %get-tuple-element.4, f32[128]{0:T(128)S(1)} %pmax.7, s32[128]{0:T(128)} %param.15, ...), kind=kOutput, calls=%fused_computation.7 | convolution fusion | flops 264918912 | bytes 6105888 | tf_op jit(solution)/shard_map/dot_general | solution.py:37
  122.3 0.0 copy-start.6
  122.3 36.2 %psum.52 = f32[128]{0:T(128)S(1)} all-reduce(f32[128]{0:T(128)S(1)} %get-tuple-element.11), channel_id=1, replica_groups=mesh['dp'=8,'vocab'=4] {'dp','vocab'}, use_global_device_ids=true, to_apply=%region_8.9 | all-reduce | flops 128 | bytes 1024 | tf_op jit(solution)/shard_map/psum | solution.py:41
  158.5 4.1 %fusion.24 = f32[128,128]{1,0:T(8,128)} fusion(f32[128,5120]{1,0:T(8,128)} %get-tuple-element.12, bf16[5120,128]{1,0:T(8,128)(2,1)} %param.13), kind=kOutput, calls=%fused_computation.38 | convolution fusion | flops 1006632960 | bytes 3997696 | tf_op jit(solution)/shard_map/dot_general | solution.py:39
  162.6 0.0 all-reduce.4.cloned.1.call-update
  162.7 0.0 copy-done.10
  162.7 0.6 dynamic_slice.7
  163.3 11.3 %all_gather.11 = f32[128,128]{1,0:T(8,128)S(1)} all-gather(f32[16,128]{1,0:T(8,128)S(1)} %get-tuple-element.6), channel_id=1, replica_groups=mesh['dp'=8,'vocab'=4] {'dp'}, dimensions={0}, use_global_device_ids=true | all-gather | bytes 73728 | tf_op jit(solution)/shard_map/all_gather | solution.py:52
  174.6 111.6 %all-reduce.4.cloned.1.call-done = f32[128,128]{1,0:T(8,128)} async-done(((f32[128,128]{1,0:T(8,128)}), f32[128,128]{1,0:T(8,128)}) %all-reduce.4.cloned.1.call-update) | async-done | bytes 65552 | tf_op jit(solution)/shard_map/psum | solution.py:41
  286.2 1.8 fusion.6
  288.0 0.0 copy-done.2
  288.0 0.2 broadcast_multiply_fusion
  288.2 0.6 convolution_convert_fusion
  288.9 1.2 fusion.25
  (21 shorter events, 0.1 us)
Async XLA Ops:
  7.2 281.7 %copy-start = (bf16[64,16384]{1,0:T(8,128)(2,1)S(1)}, bf16[64,16384]{1,0:T(8,128)(2,1)}, u32[]{:S(2)}) copy-start(bf16[64,16384]{1,0:T(8,128)(2,1)} %param.17) | copy-start | bytes 6291460
  7.2 41.8 %all-gather.2.cloned.1.call-start = ((), (), s32[]{:S(2)}) async-start(), calls=%async_computation | async-start | bytes 1474560 | tf_op jit(solution)/shard_map/all_gather | solution.py:17
  21.2 265.0 %all-reduce.4.cloned.1.call-start = ((), (), s32[]{:S(2)}) async-start(), calls=%async_computation.1 | async-start | bytes 131072 | tf_op jit(solution)/shard_map/psum | solution.py:41
  50.7 3.5 %copy-start.9 = (f32[128]{0:T(128)}, f32[128]{0:T(128)S(1)}, u32[]{:S(2)}) copy-start(f32[128]{0:T(128)S(1)} %fusion.2) | copy-start | bytes 1540
  50.7 3.4 %copy-start.7 = (f32[128]{0:T(128)}, f32[128]{0:T(128)S(1)}, u32[]{:S(2)}) copy-start(f32[128]{0:T(128)S(1)} %add_sqrt_fusion) | copy-start | bytes 1540
  50.7 41.7 %copy-start.4 = (s32[128]{0:T(128)S(1)}, s32[128]{0:T(128)}, u32[]{:S(2)}) copy-start(s32[128]{0:T(128)} %param.15) | copy-start | bytes 1540
  50.7 67.8 %copy-start.1 = (bf16[128,5120]{1,0:T(8,128)(2,1)S(1)}, bf16[128,5120]{1,0:T(8,128)(2,1)}, u32[]{:S(2)}) copy-start(bf16[128,5120]{1,0:T(8,128)(2,1)} %all-gather.2.cloned.1.call-done) | copy-start | bytes 3932164
  50.7 67.8 %copy-start.3 = (f32[5120]{0:T(1024)S(1)}, f32[5120]{0:T(1024)}, u32[]{:S(2)}) copy-start(f32[5120]{0:T(1024)} %param.11) | copy-start | bytes 61444
  118.5 3.8 %copy-start.5 = (f32[128]{0:T(128)}, f32[128]{0:T(128)S(1)}, u32[]{:S(2)}) copy-start(f32[128]{0:T(128)S(1)} %get-tuple-element.4) | copy-start | bytes 1540
  122.3 40.3 %copy-start.11 = (f32[128]{0:T(128)S(1)}, f32[128]{0:T(128)}, u32[]{:S(2)}) copy-start(f32[128]{0:T(128)} %get-tuple-element.5) | copy-start | bytes 1540
  122.3 40.3 %copy-start.10 = (f32[128]{0:T(128)S(1)}, f32[128]{0:T(128)}, u32[]{:S(2)}) copy-start(f32[128]{0:T(128)} %copy-done.9) | copy-start | bytes 1540
  122.3 40.3 %copy-start.6 = (f32[128]{0:T(128)S(1)}, f32[128]{0:T(128)}, u32[]{:S(2)}) copy-start(f32[128]{0:T(128)} %copy-done.5) | copy-start | bytes 1540
  158.5 127.7 %copy-start.8 = (f32[128]{0:T(128)S(1)}, f32[128]{0:T(128)}, u32[]{:S(2)}) copy-start(f32[128]{0:T(128)} %copy-done.7) | copy-start | bytes 1540
  162.6 125.4 %copy-start.2 = (f32[128,4]{1,0:T(8,128)S(1)}, f32[128,4]{1,0:T(8,128)}, u32[]{:S(2)}) copy-start(f32[128,4]{1,0:T(8,128)} %fusion.14) | copy-start | bytes 6148
Sparse Core Ops, SparseCore 0:
  21.3 27.6 all-gather.1
  162.8 123.3 all-reduce.3
